TPU v7x, 32 devices: a whole 2x2x4 slice. The times are simulated.
32 devices in a mesh: row: 16 (over z, y, core), col: 2 (over x).
Axes of the slice: x: 2, y: 2, z: 4, core: 2. Of those that a mesh axis runs over, the one named last changes fastest.
Arguments:
- source: float32 [4096, 2048], P('row', 'col'), may hold values from 0.25 to 4
- boxes_a: float32 [16, 8, 512, 512], P('row', 'col'), may hold values from 0.25 to 4
- shifts_a: int32 [16, 8, 2], P('row', 'col'), may hold values from -128 to -1
- widths_a: int32 [16, 8, 2], P('row', 'col'), may hold values from 256 to 512
- boxes_b: float32 [16, 8, 512, 512], P('row', 'col'), may hold values from 0.25 to 4
- shifts_b: int32 [16, 8, 2], P('row', 'col'), may hold values from -128 to -1
- widths_b: int32 [16, 8, 2], P('row', 'col'), may hold values from 256 to 512
Outputs:
- smoothed: float32 [4096, 2048], P('row', 'col')
Inputs may be any that keep to these rules, and one draw needn't show every extreme that they name: `shifts_a`: first entry: rows, second: columns. `widths_a`: first entry: rows, second: columns. `shifts_b`: first entry: rows, second: columns. `widths_b`: first entry: rows, second: columns.
All inputs are finite; a program needn't handle non-finite values.
Results may differ from a plain program's by a relative error of at most 0.0003.
Values sent between devices are 32-bit elements; how exact they have to be, the bound alone decides.
A program may use at most 64 MiB of HBM per device.

v0:
```python
import functools
import math

import jax
import jax.numpy as jnp
from jax import lax
from jax.experimental import pallas as pl
from jax.experimental.pallas import tpu as pltpu
from jax.sharding import PartitionSpec as P

S = 256
BOX = 512
ITERS = 3
RADIUS = 8
LANES = 128
HALF = S // 2
DOWN2 = HALF + RADIUS
TALL = RADIUS + 2 * S + DOWN2

kernel_eps = 0.05
blur_sigma = 2.0
blur_total = sum(
    math.exp(-(d * d) / (2.0 * blur_sigma * blur_sigma)) for d in range(-RADIUS, RADIUS + 1)
)


def gauss(offset):
    shape = (LANES, BOX + LANES)
    d = lax.broadcasted_iota(jnp.int32, shape, 1) - lax.broadcasted_iota(jnp.int32, shape, 0)
    g = gauss_of(offset - LANES + d)
    return jnp.concatenate([g[:, LANES:], g[:, :BOX]], axis=0)


def gauss_t(offset):
    shape = (BOX + LANES, LANES)
    d = lax.broadcasted_iota(jnp.int32, shape, 0) - lax.broadcasted_iota(jnp.int32, shape, 1)
    g = gauss_of(offset - LANES + d)
    return jnp.concatenate([g[LANES:], g[:BOX]], axis=1)


def gauss_of(d):
    dist = d.astype(jnp.float32) * (1.0 / S)
    return jnp.exp(dist * dist * (-1.0 / kernel_eps)).astype(jnp.bfloat16)


def blur_weight(d):
    f = d.astype(jnp.float32)
    w = jnp.exp(f * f * (-1.0 / (2.0 * blur_sigma * blur_sigma))) * (1.0 / blur_total)
    return jnp.where(jnp.abs(d) <= RADIUS, w, 0.0)


def split(x):
    hi = x.astype(jnp.bfloat16)
    return hi, (x - hi.astype(jnp.float32)).astype(jnp.bfloat16)


def dot(a, b):
    return jnp.dot(a, b, preferred_element_type=jnp.float32)


def dot_t(a, b):
    return lax.dot_general(a, b, (((1,), (1,)), ((), ())), preferred_element_type=jnp.float32)


def dot_split(a, b):
    (ah, al), (bh, bl) = a, b
    return dot(ah, bh) + (dot(ah, bl) + dot(al, bh))


def bf(x):
    return x.astype(jnp.bfloat16)


def target_of(box_ref, height, width):
    rows = lax.broadcasted_iota(jnp.int32, (BOX, BOX), 0)
    cols = lax.broadcasted_iota(jnp.int32, (BOX, BOX), 1)
    return jnp.where((rows < height) & (cols < width), box_ref[0, 0], 0.0)


MESH = pl.DeviceIdType.MESH
OWN = slice(RADIUS, RADIUS + S)


def tiles(first, count):
    return slice(first * LANES, (first + count) * LANES)


def units_of(per_dev):
    units = [(per_dev - 2, 2 * per_dev, 3)]
    units += [(j, 2 * j + 4, 2) for j in range(per_dev - 3, 0, -1)]
    units += [(0, 2 * per_dev + 3, 1), (0, 0, 3), (0, 3, 3)]
    return units


def kernel(
    per_dev,
    n_row,
    n_col,
    info,
    src,
    box_a,
    box_b,
    out,
    tgt,
    u_loc,
    mv_s,
    mv_u,
    canvas,
    bl,
    band_hi,
    band_lo,
    r1,
    r2,
    rup,
    cs,
    cl,
    s_send,
    s_recv,
    u_send,
    u_recv,
    x_send,
    x_recv,
    c_send,
    c_recv,
):
    g = pl.program_id(0)
    cols = per_dev * S
    wide = cols + 2 * S
    row, col = lax.axis_index("row"), lax.axis_index("col")
    odd = lax.rem(row, 2) == 1
    even = lax.rem(row, 2) == 0
    units = units_of(per_dev)

    def at(dr, dc):
        return (lax.rem(row + dr + n_row, n_row), lax.rem(col + dc + n_col, n_col))

    def remote(a, b, send, recv, to):
        return pltpu.make_async_remote_copy(
            src_ref=a, dst_ref=b, send_sem=send, recv_sem=recv, device_id=to, device_id_type=MESH
        )

    upper, lower = slice(0, HALF), slice(HALF, S)
    edge = slice(cols - LANES, cols)

    def halo(field, moved, k, send, recv):
        if k == 0:
            a, b, to = field.at[upper, HALF:], moved.at[lower, : cols - HALF], at(-1, 0)
        elif k == 1:
            a, b, to = field.at[upper, :LANES], moved.at[lower, edge], at(-1, -1)
        else:
            a, b, to = field.at[lower, :LANES], moved.at[upper, edge], at(0, -1)
        return remote(a, b, send.at[k], recv.at[k], to)

    def chunk(j):
        lo, hi = max(j * S, HALF), (j + 1) * S
        return remote(
            u_loc.at[upper, lo:hi],
            mv_u.at[lower, lo - HALF : hi - HALF],
            u_send.at[2 + j],
            u_recv.at[2 + j],
            at(-1, 0),
        )

    def corner(k):
        a = u_loc.at[upper, :LANES] if k == 0 else u_loc.at[lower, :LANES]
        b = mv_u.at[lower, edge] if k == 0 else mv_u.at[upper, edge]
        return remote(a, b, u_send.at[k], u_recv.at[k], at(-1, -1) if k == 0 else at(0, -1))

    def spill(n, kind):
        _, first, count = units[n]
        c = tiles(first, count)
        if kind == 0:
            a, b, to = bl.at[RADIUS + S :, c], r1.at[:, c], at(1, 0)
        elif kind == 1:
            a, b, to = bl.at[RADIUS + S : RADIUS + 2 * S, c], r1.at[:S, c], at(1, 0)
        elif kind == 2:
            a, b, to = bl.at[RADIUS + 2 * S :, c], r2.at[:, c], at(2, 0)
        else:
            a, b, to = bl.at[:RADIUS, c], rup.at[:, c], at(-1, 0)
        k = {0: 0, 1: 0, 2: 1, 3: 2}[kind]
        return remote(a, b, x_send.at[n, k], x_recv.at[n, k], to)

    def beside(k):
        if k == 0:
            a, b, to = bl.at[OWN, cols : cols + 3 * LANES], cs.at[:, : 3 * LANES], at(0, 1)
        elif k == 1:
            a, b, to = bl.at[OWN, cols + 3 * LANES :], cs.at[:, 3 * LANES :], at(0, 1)
        else:
            a, b, to = bl.at[OWN, cols + 3 * LANES :], cl, at(0, -1)
        return remote(a, b, c_send.at[k], c_recv.at[k], to)

    sides = 2 if n_col == 2 else 3

    def hand_on(n):
        @pl.when(odd)
        def _():
            c = tiles(units[n][1], units[n][2])
            spill(n, 0).wait_recv()
            bl[RADIUS + S : RADIUS + S + DOWN2, c] += r1[S:, c]
            spill(n, 1).start()
            spill(n, 2).start()

    def give(n):
        spill(n, 3).start()

        @pl.when(even)
        def _():
            spill(n, 0).start()

    def smooth(first, count):
        lo, hi = (first - 1) * LANES, (first + count + 1) * LANES
        if lo < 0:
            near = jnp.concatenate([canvas[:, wide + lo :], canvas[:, :hi]], axis=1)
        elif hi > wide:
            near = jnp.concatenate([canvas[:, lo:], canvas[:, : hi - wide]], axis=1)
        else:
            near = canvas[:, lo:hi]
        res = dot_split(split(near), [b[: (count + 2) * LANES, : count * LANES] for b in (band_hi, band_lo)])
        if first * LANES + count * LANES > wide:
            bl[:, first * LANES :] = res[:, :LANES]
            bl[:, :LANES] = res[:, LANES:]
        else:
            bl[:, tiles(first, count)] = res

    def the_band():
        n = lax.broadcasted_iota(jnp.int32, (2 * S, S), 0)
        m = lax.broadcasted_iota(jnp.int32, (2 * S, S), 1)
        return split(blur_weight(n - LANES - m))

    def folded(n, dest):
        c = tiles(units[n][1], units[n][2])

        @pl.when(even)
        def _():
            spill(n, 1).wait_recv()
            dest[...] = bl[OWN, c] + r1[:S, c]

        @pl.when(odd)
        def _():
            spill(n, 2).wait_recv()
            mine = bl[OWN, c] + r1[:S, c]
            dest[...] = mine
            dest[:DOWN2] += r2[:, c]

        spill(n, 3).wait_recv()
        dest[S - RADIUS :] += rup[:, c]

    @pl.when(g < per_dev)
    def _():
        barrier = pltpu.get_barrier_semaphore()
        peers = [(-1, 0), (1, 0), (-2, 0), (2, 0), (0, -1), (0, 1), (-1, -1), (1, 1)]

        @pl.when(g == 0)
        def _():
            for dr, dc in peers:
                pl.semaphore_signal(barrier, inc=1, device_id=at(dr, dc), device_id_type=MESH)
            mv_s[upper, : cols - HALF] = src[lower, HALF:]
            canvas[...] = jnp.zeros_like(canvas)
            band_hi[...], band_lo[...] = the_band()

        j = lax.rem(per_dev - g, per_dev)
        o_r, o_c = info[2 * j], info[2 * j + 1]
        h, w = info[2 * per_dev + 2 * j], info[2 * per_dev + 2 * j + 1]
        kr = gauss(o_r)
        krt = gauss_t(o_r)
        kc = gauss(o_c)
        tgt[...] = target_of(box_a, h, w)
        here = pl.ds(pl.multiple_of(j * S, S), S)
        a = src[:, here]
        in_r = bf(jnp.sum(krt.astype(jnp.float32), axis=1, keepdims=True)).astype(jnp.float32)
        in_c = jnp.sum(kc.astype(jnp.float32), axis=0, keepdims=True)
        back = in_r * in_c
        for step in range(ITERS):
            v = bf(tgt[...] / back)
            u = a / dot_t(bf(dot(kr, v)), kc)
            if step < ITERS - 1:
                back = dot(bf(dot(krt, bf(u))), kc)
        u_loc[:, here] = u

        @pl.when(g == 0)
        def _():
            pl.semaphore_wait(barrier, len(peers))
            for k in range(3):
                halo(src, mv_s, k, s_send, s_recv).start()
            for k in range(2):
                corner(k).start()

        for i in range(per_dev):

            @pl.when(j == i)
            def _():
                chunk(i).start()
                lo, hi = max(i * S, HALF), (i + 1) * S
                mv_u[upper, lo - HALF : hi - HALF] = u_loc[lower, lo:hi]

    @pl.when(g >= per_dev)
    def _():
        j = 2 * per_dev - 1 - g

        @pl.when(j == per_dev - 1)
        def _():
            for k in range(3):
                halo(src, mv_s, k, s_send, s_recv).wait_recv()
            for k in range(2):
                corner(k).wait_recv()

        for i in range(per_dev):

            @pl.when(j == i)
            def _():
                chunk(i).wait_recv()

        base = 4 * per_dev
        o_r, o_c = info[base + 2 * j], info[base + 2 * j + 1]
        h, w = info[base + 2 * per_dev + 2 * j], info[base + 2 * per_dev + 2 * j + 1]
        kr = gauss(o_r)
        krt = gauss_t(o_r)
        kc = gauss(o_c)
        tgt[...] = target_of(box_b, h, w)
        here = pl.ds(pl.multiple_of(j * S, S), S)
        a = mv_s[:, here]
        u = mv_u[:, here]
        for step in range(ITERS):
            back = dot(bf(dot(krt, bf(u))), kc)
            v = tgt[...] / back
            u = a / dot_t(bf(dot(kr, bf(v))), kc)
            if step == 0:
                for n, (when, _, _) in enumerate(units):
                    if when > 0:

                        @pl.when(j == when - 1)
                        def _():
                            hand_on(n)

        plan = v * dot(bf(dot(krt, bf(u))), kc)

        r = lax.broadcasted_iota(jnp.int32, (LANES, 3 * LANES), 0) - RADIUS
        m = lax.broadcasted_iota(jnp.int32, (LANES, 3 * LANES), 1) - 2 * LANES
        weights = split(blur_weight(HALF + o_r + m - r))
        halves = split(plan)
        parts = []
        for b in range(-(-TALL // LANES)):
            height = min(LANES, TALL - b * LANES)
            lo, hi = max(b - 2, 0), min(b + 1, BOX // LANES)
            wt = slice((lo - b + 2) * LANES, (hi - b + 2) * LANES)
            parts.append(
                dot_split(
                    [x[:height, wt] for x in weights],
                    [x[lo * LANES : hi * LANES] for x in halves],
                )
            )
        rowed = jnp.concatenate(parts, axis=0)
        s = HALF + o_c
        lane = lax.broadcasted_iota(jnp.int32, (TALL, LANES), 1)
        turned = [pltpu.roll(rowed[:, tiles(t, 1)], s, 1) for t in range(BOX // LANES)]
        zero = jnp.zeros((TALL, LANES), jnp.float32)
        for t in range(BOX // LANES + 1):
            left = turned[t - 1] if t > 0 else zero
            right = turned[t] if t < BOX // LANES else zero
            spot = pl.ds(pl.multiple_of(j * S + t * LANES, LANES), LANES)
            canvas[:, spot] += jnp.where(lane < s, left, right)

        for n, (when, first, count) in enumerate(units):
            if when > 0:

                @pl.when(j == when)
                def _():
                    for f in range(first, first + count, 2):
                        smooth(f, min(2, first + count - f))
                    give(n)

        @pl.when(j == 0)
        def _():
            late = [n for n, u_ in enumerate(units) if u_[0] == 0]
            corner_unit, left_unit, right_unit = late
            smooth(2 * per_dev + 3, 2)
            give(corner_unit)
            mid = units[left_unit][2]
            last = units[right_unit][1] + units[right_unit][2]
            for f in range(1, mid, 2):
                smooth(f, min(2, mid - f))
            give(left_unit)
            hand_on(corner_unit)
            for f in range(mid, last, 2):
                smooth(f, min(2, last - f))
            give(right_unit)
            hand_on(left_unit)
            hand_on(right_unit)

            folded(0, bl.at[OWN, tiles(units[0][1], units[0][2])])
            beside(0).start()
            for n in range(1, len(units) - 3):
                folded(n, out.at[:, tiles(units[n][1], units[n][2])])
            folded(corner_unit, bl.at[OWN, tiles(units[corner_unit][1], units[corner_unit][2])])
            for k in range(1, sides):
                beside(k).start()
            folded(left_unit, out.at[:, tiles(units[left_unit][1], units[left_unit][2])])
            folded(right_unit, out.at[:, tiles(units[right_unit][1], units[right_unit][2])])

            ln = lax.broadcasted_iota(jnp.int32, (S, LANES), 1)
            for k in range(sides):
                beside(k).wait_recv()
            out[:, : 3 * LANES] += cs[:, : 3 * LANES]
            out[:, 3 * LANES : 4 * LANES] += jnp.where(ln < LANES - RADIUS, cs[:, 3 * LANES :], 0.0)
            behind = cs[:, 3 * LANES :] if n_col == 2 else cl[...]
            out[:, edge] += jnp.where(ln >= LANES - RADIUS, behind, 0.0)

            for k in range(3):
                halo(src, mv_s, k, s_send, s_recv).wait_send()
            for k in range(2):
                corner(k).wait_send()
            for i in range(per_dev):
                chunk(i).wait_send()
            for k in range(sides):
                beside(k).wait_send()
            for n in range(len(units)):
                spill(n, 3).wait_send()

                @pl.when(even)
                def _():
                    spill(n, 0).wait_send()

                @pl.when(odd)
                def _():
                    spill(n, 1).wait_send()
                    spill(n, 2).wait_send()


def on_device(n_row, n_col, source, boxes_a, shifts_a, widths_a, boxes_b, shifts_b, widths_b):
    cols = source.shape[1]
    per_dev = cols // S
    wide = cols + 2 * S
    units = len(units_of(per_dev))
    info = jnp.concatenate([shifts_a, widths_a, shifts_b, widths_b]).reshape(-1)
    f32 = lambda *shape: pltpu.VMEM(shape, jnp.float32)
    dma = pltpu.SemaphoreType.DMA
    box = (1, 1, BOX, BOX)
    first = lambda g, *_: (0, lax.rem(per_dev - jnp.minimum(g, per_dev - 1), per_dev), 0, 0)
    second = lambda g, *_: (0, jnp.minimum(2 * per_dev - 1 - g, per_dev - 1), 0, 0)
    return pl.pallas_call(
        functools.partial(kernel, per_dev, n_row, n_col),
        grid_spec=pltpu.PrefetchScalarGridSpec(
            num_scalar_prefetch=1,
            grid=(2 * per_dev,),
            in_specs=[
                pl.BlockSpec((S, cols), lambda g, *_: (0, 0)),
                pl.BlockSpec(box, first),
                pl.BlockSpec(box, second),
            ],
            out_specs=pl.BlockSpec((S, cols), lambda g, *_: (0, 0)),
            scratch_shapes=[
                f32(BOX, BOX),
                f32(S, cols),
                f32(S, cols),
                f32(S, cols),
                f32(TALL, wide),
                f32(TALL, wide),
                pltpu.VMEM((2 * S, S), jnp.bfloat16),
                pltpu.VMEM((2 * S, S), jnp.bfloat16),
                f32(S + DOWN2, wide),
                f32(DOWN2, wide),
                f32(RADIUS, wide),
                f32(S, 2 * S),
                f32(S, LANES),
                dma((3,)),
                dma((3,)),
                dma((2 + per_dev,)),
                dma((2 + per_dev,)),
                dma((units, 3)),
                dma((units, 3)),
                dma((3,)),
                dma((3,)),
            ],
        ),
        out_shape=jax.ShapeDtypeStruct((S, cols), jnp.float32),
        compiler_params=pltpu.CompilerParams(
            vmem_limit_bytes=56 * 1024 * 1024, collective_id=0, has_side_effects=True
        ),
        name="transport",
    )(info, source, boxes_a, boxes_b)


def solution(mesh):
    return jax.shard_map(
        functools.partial(on_device, mesh.shape["row"], mesh.shape["col"]),
        mesh=mesh,
        in_specs=(
            P("row", "col"),
            P("row", "col", None, None),
            P("row", "col", None),
            P("row", "col", None),
            P("row", "col", None, None),
            P("row", "col", None),
            P("row", "col", None),
        ),
        out_specs=P("row", "col"),
        check_vma=False,
    )
```

profile of v0, /device:TPU:1, one launch (start us, length us, event | category | flops | bytes accessed | tf_op | source)
XLA Modules:
  0.0 66.2 jit_solution(2425002338968056917)
XLA Ops:
  0.0 0.7 %pad_add_fusion = s32[4,4,2]{1,2,0:T(2,128)S(1)} fusion(s32[1,4,2]{1,2,0:T(2,128)} %param.13, s32[1,4,2]{1,2,0:T(2,128)} %param.12, s32[1,4,2]{1,2,0:T(2,128)} %param.10, s32[1,4,2]{1,2,0:T(2,128)} %param.9), kind=kLoop, calls=%fused_computation | loop fusion | flops 96 | bytes 256 | tf_op jit(solution)/shard_map/concatenate | solution.py:434
  0.7 0.1 copy.9
  0.8 0.6 reshape.3.info
  1.5 62.4 %transport.1 = f32[256,1024]{1,0:T(8,128)} custom-call(s32[32]{0:T(128)} %reshape.3.info, f32[256,1024]{1,0:T(8,128)} %src.1, f32[1,4,512,512]{3,2,1,0:T(8,128)} %box_a.1, f32[1,4,512,512]{3,2,1,0:T(8,128)} %box_b.1), custom_call_target="tpu_custom_call" | custom-call | tf_op jit(solution)/shard_map/transport/pallas_call | solution.py:440
  63.9 2.3 %copy.11 = f32[256,1024]{1,0:T(8,128)} copy(f32[256,1024]{1,0:T(8,128)} %transport.1) | data formatting | bytes 2097152
where the time goes:
time: 66.4 us; the launch traced here: 66.2 us
  Pallas kernels  62.4 us (94%)
  local copies, waits for them, and re-layouts  3.03 us (5%)
  other arithmetic  0.73 us (1%)
    pallas_call x1, Pallas kernels, on_device(): pl.pallas_call(functools.partial(kernel, per_dev, n_row, n_col), grid_spe...  62.4 us
    unnamed x1, local copies, waits for them, and re-layouts  2.31 us

commit v1 on v0

v1 whole, which is shorter than its diff:
```python
import functools
import math

import jax
import jax.numpy as jnp
from jax import lax
from jax.experimental import pallas as pl
from jax.experimental.pallas import tpu as pltpu
from jax.sharding import PartitionSpec as P

S = 256
BOX = 512
ITERS = 3
RADIUS = 8
LANES = 128
HALF = S // 2
DOWN2 = HALF + RADIUS
TALL = RADIUS + 2 * S + DOWN2

kernel_eps = 0.05
blur_sigma = 2.0
blur_total = sum(
    math.exp(-(d * d) / (2.0 * blur_sigma * blur_sigma)) for d in range(-RADIUS, RADIUS + 1)
)


def gauss(offset):
    shape = (LANES, BOX + LANES)
    d = lax.broadcasted_iota(jnp.int32, shape, 1) - lax.broadcasted_iota(jnp.int32, shape, 0)
    g = gauss_of(offset - LANES + d)
    return jnp.concatenate([g[:, LANES:], g[:, :BOX]], axis=0)


def gauss_t(offset):
    shape = (BOX + LANES, LANES)
    d = lax.broadcasted_iota(jnp.int32, shape, 0) - lax.broadcasted_iota(jnp.int32, shape, 1)
    g = gauss_of(offset - LANES + d)
    return jnp.concatenate([g[LANES:], g[:BOX]], axis=1)


def gauss_of(d):
    dist = d.astype(jnp.float32) * (1.0 / S)
    return jnp.exp(dist * dist * (-1.0 / kernel_eps)).astype(jnp.bfloat16)


def blur_weight(d):
    f = d.astype(jnp.float32)
    w = jnp.exp(f * f * (-1.0 / (2.0 * blur_sigma * blur_sigma))) * (1.0 / blur_total)
    return jnp.where(jnp.abs(d) <= RADIUS, w, 0.0)


def split(x):
    hi = x.astype(jnp.bfloat16)
    return hi, (x - hi.astype(jnp.float32)).astype(jnp.bfloat16)


def dot(a, b):
    return jnp.dot(a, b, preferred_element_type=jnp.float32)


def dot_t(a, b):
    return lax.dot_general(a, b, (((1,), (1,)), ((), ())), preferred_element_type=jnp.float32)


def dot_split(a, b):
    (ah, al), (bh, bl) = a, b
    return dot(ah, bh) + (dot(ah, bl) + dot(al, bh))


def bf(x):
    return x.astype(jnp.bfloat16)


def target_of(box_ref, height, width):
    rows = lax.broadcasted_iota(jnp.int32, (BOX, BOX), 0)
    cols = lax.broadcasted_iota(jnp.int32, (BOX, BOX), 1)
    return jnp.where((rows < height) & (cols < width), box_ref[0, 0], 0.0)


MESH = pl.DeviceIdType.MESH
OWN = slice(RADIUS, RADIUS + S)


def tiles(first, count):
    return slice(first * LANES, (first + count) * LANES)


def plan_of(per_dev):
    last = per_dev - 1
    a_order = list(dict.fromkeys([0, last, min(1, last)] + list(range(per_dev - 2, 1, -1))))
    b_order = list(dict.fromkeys([last, 0] + list(range(per_dev - 2, 0, -1))))
    steps = [("a", j) for j in a_order[:3]]
    a_left, b_left = a_order[3:], list(b_order)
    while b_left:
        steps.append(("b", b_left.pop(0)))
        if a_left:
            steps.append(("a", a_left.pop(0)))
    n_tiles = 2 * per_dev + 3
    done, units, sent = [], [], set()
    for g, (kind, j) in enumerate(steps):
        if kind == "a":
            continue
        done.append(j)
        ready = [
            t
            for t in range(n_tiles)
            if t not in sent
            and all(i in done for i in range(per_dev) if 2 * i <= t <= 2 * i + 4)
        ]
        sent.update(ready)
        runs = []
        for t in reversed(ready):
            if runs and runs[-1][0] == t + 1 and runs[-1][1] < 3:
                runs[-1] = (t, runs[-1][1] + 1)
            else:
                runs.append((t, 1))
        units += [(g, first, count) for first, count in runs]
    return steps, units


def kernel(
    per_dev,
    n_row,
    n_col,
    shifts_a,
    widths_a,
    shifts_b,
    widths_b,
    src,
    box_a,
    box_b,
    out,
    tgt,
    u_loc,
    mv_s,
    mv_u,
    canvas,
    band_hi,
    band_lo,
    r1,
    r2,
    rup,
    sb,
    cs,
    cl,
    s_send,
    s_recv,
    u_send,
    u_recv,
    x_send,
    x_recv,
    c_send,
    c_recv,
):
    g = pl.program_id(0)
    cols = per_dev * S
    n_tiles = 2 * per_dev + 3
    row, col = lax.axis_index("row"), lax.axis_index("col")
    odd = lax.rem(row, 2) == 1
    even = lax.rem(row, 2) == 0
    steps, units = plan_of(per_dev)
    n_steps = len(steps)

    def pick(values):
        res = jnp.int32(values[0])
        for k in range(1, n_steps):
            res = jnp.where(g == k, jnp.int32(values[k]), res)
        return res

    j = pick([c for _, c in steps])
    is_a = pick([int(k == "a") for k, _ in steps]) == 1

    def at(dr, dc):
        return (lax.rem(row + dr + n_row, n_row), lax.rem(col + dc + n_col, n_col))

    def remote(a, b, send, recv, to):
        return pltpu.make_async_remote_copy(
            src_ref=a, dst_ref=b, send_sem=send, recv_sem=recv, device_id=to, device_id_type=MESH
        )

    upper, lower = slice(0, HALF), slice(HALF, S)
    edge = slice(cols - LANES, cols)

    def halo(field, moved, k, send, recv):
        if k == 0:
            a, b, to = field.at[upper, HALF:], moved.at[lower, : cols - HALF], at(-1, 0)
        elif k == 1:
            a, b, to = field.at[upper, :LANES], moved.at[lower, edge], at(-1, -1)
        else:
            a, b, to = field.at[lower, :LANES], moved.at[upper, edge], at(0, -1)
        return remote(a, b, send.at[k], recv.at[k], to)

    def chunk(j):
        lo, hi = max(j * S, HALF), (j + 1) * S
        return remote(
            u_loc.at[upper, lo:hi],
            mv_u.at[lower, lo - HALF : hi - HALF],
            u_send.at[2 + j],
            u_recv.at[2 + j],
            at(-1, 0),
        )

    def corner(k):
        a = u_loc.at[upper, :LANES] if k == 0 else u_loc.at[lower, :LANES]
        b = mv_u.at[lower, edge] if k == 0 else mv_u.at[upper, edge]
        return remote(a, b, u_send.at[k], u_recv.at[k], at(-1, -1) if k == 0 else at(0, -1))

    near, far = RADIUS + S, RADIUS + 2 * S
    mid = near + DOWN2

    def spill(n, kind):
        _, first, count = units[n]
        c = tiles(first, count)
        a, b, to, k = {
            "even_far": (canvas.at[far:, c], r1.at[S:, c], at(1, 0), 0),
            "even_near": (canvas.at[near:far, c], r1.at[:S, c], at(1, 0), 1),
            "odd_near": (canvas.at[near:mid, c], r1.at[:DOWN2, c], at(1, 0), 0),
            "odd_mid": (canvas.at[mid:far, c], r1.at[DOWN2:S, c], at(1, 0), 1),
            "odd_far": (canvas.at[far:, c], r2.at[:, c], at(2, 0), 2),
            "up": (canvas.at[:RADIUS, c], rup.at[:, c], at(-1, 0), 3),
        }[kind]
        return remote(a, b, x_send.at[n, k], x_recv.at[n, k], to)

    flank = slice(0, 3 * LANES)
    tip = slice(3 * LANES, 4 * LANES)

    def beside(k):
        if k == 0:
            a, b, to = sb.at[:, flank], cs.at[:, flank], at(0, 1)
        elif k == 1:
            a, b, to = sb.at[:, tip], cs.at[:, tip], at(0, 1)
        else:
            a, b, to = sb.at[:, tip], cl, at(0, -1)
        return remote(a, b, c_send.at[k], c_recv.at[k], to)

    sides = 2 if n_col == 2 else 3

    def give(n):
        @pl.when(even)
        def _():
            spill(n, "even_far").start()
            spill(n, "even_near").start()

        @pl.when(odd)
        def _():
            spill(n, "odd_far").start()
            spill(n, "odd_mid").start()

        spill(n, "up").start()

    def hand_on(n):
        @pl.when(odd)
        def _():
            c = tiles(units[n][1], units[n][2])
            spill(n, "even_far").wait_recv()
            canvas[near:mid, c] += r1[S:, c]
            spill(n, "odd_near").start()

    def between():
        for k in range(1, n_steps):
            ready = [n for n, u in enumerate(units) if u[0] == k - 1]
            if ready:

                @pl.when(g == k)
                def _():
                    for n in ready:
                        hand_on(n)

    def fold(n):
        c = tiles(units[n][1], units[n][2])

        @pl.when(even)
        def _():
            spill(n, "odd_near").wait_recv()
            spill(n, "odd_mid").wait_recv()
            canvas[OWN, c] += r1[:S, c]

        @pl.when(odd)
        def _():
            spill(n, "even_near").wait_recv()
            spill(n, "odd_far").wait_recv()
            canvas[OWN, c] += r1[:S, c]
            canvas[RADIUS : RADIUS + DOWN2, c] += r2[:, c]

        spill(n, "up").wait_recv()
        canvas[S : RADIUS + S, c] += rup[:, c]

    def smooth(first, count):
        lo, hi = max(first - 1, 0), min(first + count + 1, n_tiles)
        rows = slice((lo - first + 1) * LANES, (hi - first + 1) * LANES)
        field = split(canvas[OWN, lo * LANES : hi * LANES])
        return dot_split(field, [b[rows, : count * LANES] for b in (band_hi, band_lo)])

    def the_band():
        n = lax.broadcasted_iota(jnp.int32, (2 * S, S), 0)
        m = lax.broadcasted_iota(jnp.int32, (2 * S, S), 1)
        return split(blur_weight(n - LANES - m))

    @pl.when(is_a)
    def _():
        barrier = pltpu.get_barrier_semaphore()
        peers = [(-1, 0), (1, 0), (-2, 0), (2, 0), (0, -1), (0, 1), (-1, -1), (1, 1)]

        @pl.when(g == 0)
        def _():
            for dr, dc in peers:
                pl.semaphore_signal(barrier, inc=1, device_id=at(dr, dc), device_id_type=MESH)
            mv_s[upper, : cols - HALF] = src[lower, HALF:]
            canvas[...] = jnp.zeros_like(canvas)
            band_hi[...], band_lo[...] = the_band()

        o_r, o_c = shifts_a[0, 0, j], shifts_a[0, 1, j]
        h, w = widths_a[0, 0, j], widths_a[0, 1, j]
        kr = gauss(o_r)
        krt = gauss_t(o_r)
        kc = gauss(o_c)
        tgt[...] = target_of(box_a, h, w)
        here = pl.ds(pl.multiple_of(j * S, S), S)
        a = src[:, here]
        in_r = bf(jnp.sum(krt.astype(jnp.float32), axis=1, keepdims=True)).astype(jnp.float32)
        in_c = jnp.sum(kc.astype(jnp.float32), axis=0, keepdims=True)
        back = in_r * in_c
        for step in range(ITERS):
            v = bf(tgt[...] / back)
            u = a / dot_t(bf(dot(kr, v)), kc)
            if step < ITERS - 1:
                back = dot(bf(dot(krt, bf(u))), kc)
            if step == 0:

                @pl.when(g == 0)
                def _():
                    pl.semaphore_wait(barrier, len(peers))
                    for k in range(3):
                        halo(src, mv_s, k, s_send, s_recv).start()

                between()
        u_loc[:, here] = u

        @pl.when(g == 0)
        def _():
            for k in range(2):
                corner(k).start()

        for i in range(per_dev):

            @pl.when(j == i)
            def _():
                chunk(i).start()
                lo, hi = max(i * S, HALF), (i + 1) * S
                mv_u[upper, lo - HALF : hi - HALF] = u_loc[lower, lo:hi]

    @pl.when(jnp.logical_not(is_a))
    def _():
        waited = set()
        for k, (kind, i) in enumerate(steps):
            if kind == "a":
                continue
            need = [c for c in (i, i + 1) if c < per_dev and c not in waited]
            waited.update(need)

            @pl.when(g == k)
            def _():
                if len(waited) == len(need):
                    halo(src, mv_s, 0, s_send, s_recv).wait_recv()
                if i == per_dev - 1:
                    for c in range(1, 3):
                        halo(src, mv_s, c, s_send, s_recv).wait_recv()
                    for c in range(2):
                        corner(c).wait_recv()
                for c in need:
                    chunk(c).wait_recv()

        o_r, o_c = shifts_b[0, 0, j], shifts_b[0, 1, j]
        h, w = widths_b[0, 0, j], widths_b[0, 1, j]
        kr = gauss(o_r)
        krt = gauss_t(o_r)
        kc = gauss(o_c)
        tgt[...] = target_of(box_b, h, w)
        here = pl.ds(pl.multiple_of(j * S, S), S)
        a = mv_s[:, here]
        u = mv_u[:, here]
        for step in range(ITERS):
            back = dot(bf(dot(krt, bf(u))), kc)
            v = tgt[...] / back
            u = a / dot_t(bf(dot(kr, bf(v))), kc)
            if step == 0:
                between()

        plan = v * dot(bf(dot(krt, bf(u))), kc)

        r = lax.broadcasted_iota(jnp.int32, (LANES, 3 * LANES), 0) - RADIUS
        m = lax.broadcasted_iota(jnp.int32, (LANES, 3 * LANES), 1) - 2 * LANES
        weights = split(blur_weight(HALF + o_r + m - r))
        halves = split(plan)
        parts = []
        for b in range(-(-TALL // LANES)):
            height = min(LANES, TALL - b * LANES)
            lo, hi = max(b - 2, 0), min(b + 1, BOX // LANES)
            wt = slice((lo - b + 2) * LANES, (hi - b + 2) * LANES)
            parts.append(
                dot_split(
                    [x[:height, wt] for x in weights],
                    [x[lo * LANES : hi * LANES] for x in halves],
                )
            )
        rowed = jnp.concatenate(parts, axis=0)
        s = HALF + o_c
        lane = lax.broadcasted_iota(jnp.int32, (TALL, LANES), 1)
        turned = [pltpu.roll(rowed[:, tiles(t, 1)], s, 1) for t in range(BOX // LANES)]
        zero = jnp.zeros((TALL, LANES), jnp.float32)
        for t in range(BOX // LANES + 1):
            left = turned[t - 1] if t > 0 else zero
            right = turned[t] if t < BOX // LANES else zero
            spot = pl.ds(pl.multiple_of(j * S + t * LANES, LANES), LANES)
            canvas[:, spot] += jnp.where(lane < s, left, right)

        for k in range(n_steps):
            ready = [n for n, u_ in enumerate(units) if u_[0] == k]
            if ready:

                @pl.when(g == k)
                def _():
                    for n in ready:
                        give(n)

        @pl.when(g == n_steps - 1)
        def _():
            final = [n for n, u_ in enumerate(units) if u_[0] == n_steps - 1]
            early = [n for n in range(len(units)) if n not in final]
            fold(early[0])
            for n in final:
                hand_on(n)
            for n in early[1:]:
                fold(n)

            first = 2 * per_dev
            sb[:, 2 * LANES : 3 * LANES] = smooth(first + 2, 1)
            sb[:, : 2 * LANES] = smooth(first, 2)
            over = split(canvas[OWN, tiles(n_tiles - 1, 1)])
            under = split(canvas[OWN, tiles(0, 1)])
            sb[:, tip] = dot_split(over, [b[:LANES, :LANES] for b in (band_hi, band_lo)]) + dot_split(
                under, [b[2 * LANES : 3 * LANES, :LANES] for b in (band_hi, band_lo)]
            )
            for k in range(sides):
                beside(k).start()

            ready = set()
            for n in early:
                ready.update(range(units[n][1], units[n][1] + units[n][2]))
            shown = set()

            def show():
                t = 2 * per_dev - 1
                while t >= 0:
                    ok = lambda x: x not in shown and all(
                        y in ready for y in (x - 1, x, x + 1) if 0 <= y < n_tiles
                    )
                    if ok(t):
                        count = 2 if t > 0 and ok(t - 1) else 1
                        base = t - count + 1
                        out[:, tiles(base, count)] = smooth(base, count)
                        shown.update(range(base, t + 1))
                        t -= count
                    else:
                        t -= 1

            show()
            for n in final:
                fold(n)
                ready.update(range(units[n][1], units[n][1] + units[n][2]))
                show()

            ln = lax.broadcasted_iota(jnp.int32, (S, LANES), 1)
            for k in range(sides):
                beside(k).wait_recv()
            out[:, flank] += cs[:, flank]
            out[:, tip] += jnp.where(ln < LANES - RADIUS, cs[:, tip], 0.0)
            behind = cs[:, tip] if n_col == 2 else cl[...]
            out[:, edge] += jnp.where(ln >= LANES - RADIUS, behind, 0.0)

            for k in range(3):
                halo(src, mv_s, k, s_send, s_recv).wait_send()
            for k in range(2):
                corner(k).wait_send()
            for i in range(per_dev):
                chunk(i).wait_send()
            for k in range(sides):
                beside(k).wait_send()
            for n in range(len(units)):
                spill(n, "up").wait_send()

                @pl.when(even)
                def _():
                    spill(n, "even_far").wait_send()
                    spill(n, "even_near").wait_send()

                @pl.when(odd)
                def _():
                    spill(n, "odd_near").wait_send()
                    spill(n, "odd_mid").wait_send()
                    spill(n, "odd_far").wait_send()


def on_device(n_row, n_col, source, boxes_a, shifts_a, widths_a, boxes_b, shifts_b, widths_b):
    cols = source.shape[1]
    per_dev = cols // S
    wide = cols + 3 * LANES
    steps, units = plan_of(per_dev)
    f32 = lambda *shape: pltpu.VMEM(shape, jnp.float32)
    dma = pltpu.SemaphoreType.DMA
    box = (1, 1, BOX, BOX)

    def boxes_of(kind):
        def where(g):
            block = None
            for k in range(len(steps) - 1, -1, -1):
                if steps[k][0] != kind:
                    continue
                block = jnp.int32(steps[k][1]) if block is None else jnp.where(g <= k, steps[k][1], block)
            return (0, block, 0, 0)

        return pl.BlockSpec(box, where)

    smem = pl.BlockSpec(memory_space=pltpu.SMEM)
    return pl.pallas_call(
        functools.partial(kernel, per_dev, n_row, n_col),
        grid_spec=pltpu.PrefetchScalarGridSpec(
            num_scalar_prefetch=0,
            grid=(len(steps),),
            in_specs=[
                smem,
                smem,
                smem,
                smem,
                pl.BlockSpec((S, cols), lambda g: (0, 0)),
                boxes_of("a"),
                boxes_of("b"),
            ],
            out_specs=pl.BlockSpec((S, cols), lambda g: (0, 0)),
            scratch_shapes=[
                f32(BOX, BOX),
                f32(S, cols),
                f32(S, cols),
                f32(S, cols),
                f32(TALL, wide),
                pltpu.VMEM((2 * S, S), jnp.bfloat16),
                pltpu.VMEM((2 * S, S), jnp.bfloat16),
                f32(S + DOWN2, wide),
                f32(DOWN2, wide),
                f32(RADIUS, wide),
                f32(S, 4 * LANES),
                f32(S, 4 * LANES),
                f32(S, LANES),
                dma((3,)),
                dma((3,)),
                dma((2 + per_dev,)),
                dma((2 + per_dev,)),
                dma((len(units), 4)),
                dma((len(units), 4)),
                dma((3,)),
                dma((3,)),
            ],
        ),
        out_shape=jax.ShapeDtypeStruct((S, cols), jnp.float32),
        compiler_params=pltpu.CompilerParams(
            vmem_limit_bytes=56 * 1024 * 1024, collective_id=0, has_side_effects=True
        ),
        name="transport",
    )(*[x.swapaxes(1, 2) for x in (shifts_a, widths_a, shifts_b, widths_b)], source, boxes_a, boxes_b)


def solution(mesh):
    return jax.shard_map(
        functools.partial(on_device, mesh.shape["row"], mesh.shape["col"]),
        mesh=mesh,
        in_specs=(
            P("row", "col"),
            P("row", "col", None, None),
            P("row", "col", None),
            P("row", "col", None),
            P("row", "col", None, None),
            P("row", "col", None),
            P("row", "col", None),
        ),
        out_specs=P("row", "col"),
        check_vma=False,
    )
```

time: 66.4 us -> 60.1 us (0.905)
  the two profiles are of different devices: /device:TPU:1 before, /device:TPU:0 now
where the time goes in v1:
time: 60.1 us; the launch traced here: 60 us
  Pallas kernels  57.6 us (96%)
  local copies, waits for them, and re-layouts  2.31 us (4%)
    pallas_call x1, Pallas kernels, on_device(): pl.pallas_call(functools.partial(kernel, per_dev, n_row, n_col), grid_spe...  57.6 us
    unnamed x1, local copies, waits for them, and re-layouts  2.31 us

profile of v1, /device:TPU:0, one launch (start us, length us, event | category | flops | bytes accessed | tf_op | source)
XLA Modules:
  0.0 60.0 jit_solution(5561168905742678850)
XLA Ops:
  0.0 57.6 %transport.1 = f32[256,1024]{1,0:T(8,128)} custom-call(s32[1,2,4]{2,1,0:T(2,128)} %bitcast.4, s32[1,2,4]{2,1,0:T(2,128)} %bitcast.5, s32[1,2,4]{2,1,0:T(2,128)} %bitcast.6, s32[1,2,4]{2,1,0:T(2,128)} %bitcast.7, f32[256,1024]{1,0:T(8,128)} %src.1, f32[1,4,512,512]{3,2,1,0:T(8,128)} %box_a.1, f32[1,4,512,512]{3,2,1,0:T(8,128)} %box_b.1), custom_call_target="tpu_custom_call" | custom-call | tf_op jit(solution)/shard_map/transport/pallas_call | solution.py:525
  57.7 2.3 %copy.9 = f32[256,1024]{1,0:T(8,128)} copy(f32[256,1024]{1,0:T(8,128)} %transport.1) | data formatting | bytes 2097152

commit v2 on v1

--- a/solution.py
+++ b/solution.py
@@ -89,18 +89,14 @@
     last = per_dev - 1
     a_order = list(dict.fromkeys([0, last, min(1, last)] + list(range(per_dev - 2, 1, -1))))
     b_order = list(dict.fromkeys([last, 0] + list(range(per_dev - 2, 0, -1))))
-    steps = [("a", j) for j in a_order[:3]]
-    a_left, b_left = a_order[3:], list(b_order)
-    while b_left:
-        steps.append(("b", b_left.pop(0)))
-        if a_left:
-            steps.append(("a", a_left.pop(0)))
+    steps = [("a", tuple(a_order[k : k + 2])) for k in range(0, per_dev, 2)]
+    steps += [("b", (j,)) for j in b_order]
     n_tiles = 2 * per_dev + 3
     done, units, sent = [], [], set()
-    for g, (kind, j) in enumerate(steps):
+    for g, (kind, cells) in enumerate(steps):
         if kind == "a":
             continue
-        done.append(j)
+        done += cells
         ready = [
             t
             for t in range(n_tiles)
@@ -128,9 +124,11 @@
     widths_b,
     src,
     box_a,
+    box_c,
     box_b,
     out,
     tgt,
+    tgt_c,
     u_loc,
     mv_s,
     mv_u,
@@ -167,7 +165,7 @@
             res = jnp.where(g == k, jnp.int32(values[k]), res)
         return res
 
-    j = pick([c for _, c in steps])
+    j, j_c = pick([c[0] for _, c in steps]), pick([c[-1] for _, c in steps])
     is_a = pick([int(k == "a") for k, _ in steps]) == 1
 
     def at(dr, dc):
@@ -183,27 +181,19 @@
 
     def halo(field, moved, k, send, recv):
         if k == 0:
-            a, b, to = field.at[upper, HALF:], moved.at[lower, : cols - HALF], at(-1, 0)
+            a, b, to = field.at[upper, :LANES], moved.at[lower, edge], at(-1, -1)
         elif k == 1:
-            a, b, to = field.at[upper, :LANES], moved.at[lower, edge], at(-1, -1)
+            a, b, to = field.at[lower, :LANES], moved.at[upper, edge], at(0, -1)
         else:
-            a, b, to = field.at[lower, :LANES], moved.at[upper, edge], at(0, -1)
+            lo, hi = max((k - 2) * S, HALF), (k - 1) * S
+            a, b, to = field.at[upper, lo:hi], moved.at[lower, lo - HALF : hi - HALF], at(-1, 0)
         return remote(a, b, send.at[k], recv.at[k], to)
 
-    def chunk(j):
-        lo, hi = max(j * S, HALF), (j + 1) * S
-        return remote(
-            u_loc.at[upper, lo:hi],
-            mv_u.at[lower, lo - HALF : hi - HALF],
-            u_send.at[2 + j],
-            u_recv.at[2 + j],
-            at(-1, 0),
-        )
-
-    def corner(k):
-        a = u_loc.at[upper, :LANES] if k == 0 else u_loc.at[lower, :LANES]
-        b = mv_u.at[lower, edge] if k == 0 else mv_u.at[upper, edge]
-        return remote(a, b, u_send.at[k], u_recv.at[k], at(-1, -1) if k == 0 else at(0, -1))
+    def mass(k):
+        return halo(src, mv_s, k, s_send, s_recv)
+
+    def scale(k):
+        return halo(u_loc, mv_u, k, u_send, u_recv)
 
     near, far = RADIUS + S, RADIUS + 2 * S
     mid = near + DOWN2
@@ -309,66 +299,69 @@
             canvas[...] = jnp.zeros_like(canvas)
             band_hi[...], band_lo[...] = the_band()
 
-        o_r, o_c = shifts_a[0, 0, j], shifts_a[0, 1, j]
-        h, w = widths_a[0, 0, j], widths_a[0, 1, j]
-        kr = gauss(o_r)
-        krt = gauss_t(o_r)
-        kc = gauss(o_c)
-        tgt[...] = target_of(box_a, h, w)
-        here = pl.ds(pl.multiple_of(j * S, S), S)
-        a = src[:, here]
-        in_r = bf(jnp.sum(krt.astype(jnp.float32), axis=1, keepdims=True)).astype(jnp.float32)
-        in_c = jnp.sum(kc.astype(jnp.float32), axis=0, keepdims=True)
-        back = in_r * in_c
+        cells = []
+        for c, box, t in ((j, box_a, tgt), (j_c, box_c, tgt_c)):
+            o_r, o_c = shifts_a[0, 0, c], shifts_a[0, 1, c]
+            h, w = widths_a[0, 0, c], widths_a[0, 1, c]
+            krt, kc = gauss_t(o_r), gauss(o_c)
+            t[...] = target_of(box, h, w)
+            here = pl.ds(pl.multiple_of(c * S, S), S)
+            in_r = bf(jnp.sum(krt.astype(jnp.float32), axis=1, keepdims=True)).astype(jnp.float32)
+            in_c = jnp.sum(kc.astype(jnp.float32), axis=0, keepdims=True)
+            cells.append((gauss(o_r), krt, kc, t, src[:, here], here, in_r * in_c))
+        back = [c[-1] for c in cells]
         for step in range(ITERS):
-            v = bf(tgt[...] / back)
-            u = a / dot_t(bf(dot(kr, v)), kc)
+            v = [bf(c[3][...] / b) for c, b in zip(cells, back)]
+            inner = [bf(dot(c[0], x)) for c, x in zip(cells, v)]
+            u = [c[4] / dot_t(x, c[2]) for c, x in zip(cells, inner)]
             if step < ITERS - 1:
-                back = dot(bf(dot(krt, bf(u))), kc)
+                inner = [bf(dot(c[1], bf(x))) for c, x in zip(cells, u)]
+                back = [dot(x, c[2]) for c, x in zip(cells, inner)]
             if step == 0:
 
                 @pl.when(g == 0)
                 def _():
                     pl.semaphore_wait(barrier, len(peers))
-                    for k in range(3):
-                        halo(src, mv_s, k, s_send, s_recv).start()
-
-                between()
-        u_loc[:, here] = u
-
-        @pl.when(g == 0)
-        def _():
-            for k in range(2):
-                corner(k).start()
-
-        for i in range(per_dev):
-
-            @pl.when(j == i)
+                    for k in (0, 1, 1 + per_dev, 2):
+                        mass(k).start()
+
+        for c, x in zip(cells, u):
+            u_loc[:, c[5]] = x
+
+        for n, (kind, pair) in enumerate(steps):
+            if kind == "b":
+                continue
+
+            @pl.when(g == n)
             def _():
-                chunk(i).start()
-                lo, hi = max(i * S, HALF), (i + 1) * S
-                mv_u[upper, lo - HALF : hi - HALF] = u_loc[lower, lo:hi]
+                if n == 0:
+                    scale(0).start()
+                    scale(1).start()
+                for i in reversed(pair):
+                    scale(2 + i).start()
+                if n == 0:
+                    for k in range(per_dev, 2, -1):
+                        mass(k).start()
+                for i in pair:
+                    lo, hi = max(i * S, HALF), (i + 1) * S
+                    mv_u[upper, lo - HALF : hi - HALF] = u_loc[lower, lo:hi]
 
     @pl.when(jnp.logical_not(is_a))
     def _():
         waited = set()
-        for k, (kind, i) in enumerate(steps):
+        for k, (kind, pair) in enumerate(steps):
             if kind == "a":
                 continue
-            need = [c for c in (i, i + 1) if c < per_dev and c not in waited]
+            (i,) = pair
+            need = [2 + c for c in (i, i + 1) if c < per_dev]
+            need = [c for c in need + [0, 1] * (i == per_dev - 1) if c not in waited]
             waited.update(need)
 
             @pl.when(g == k)
             def _():
-                if len(waited) == len(need):
-                    halo(src, mv_s, 0, s_send, s_recv).wait_recv()
-                if i == per_dev - 1:
-                    for c in range(1, 3):
-                        halo(src, mv_s, c, s_send, s_recv).wait_recv()
-                    for c in range(2):
-                        corner(c).wait_recv()
                 for c in need:
-                    chunk(c).wait_recv()
+                    mass(c).wait_recv()
+                    scale(c).wait_recv()
 
         o_r, o_c = shifts_b[0, 0, j], shifts_b[0, 1, j]
         h, w = widths_b[0, 0, j], widths_b[0, 1, j]
@@ -478,12 +471,9 @@
             behind = cs[:, tip] if n_col == 2 else cl[...]
             out[:, edge] += jnp.where(ln >= LANES - RADIUS, behind, 0.0)
 
-            for k in range(3):
-                halo(src, mv_s, k, s_send, s_recv).wait_send()
-            for k in range(2):
-                corner(k).wait_send()
-            for i in range(per_dev):
-                chunk(i).wait_send()
+            for k in range(2 + per_dev):
+                mass(k).wait_send()
+                scale(k).wait_send()
             for k in range(sides):
                 beside(k).wait_send()
             for n in range(len(units)):
@@ -510,13 +500,14 @@
     dma = pltpu.SemaphoreType.DMA
     box = (1, 1, BOX, BOX)
 
-    def boxes_of(kind):
+    def boxes_of(kind, side):
         def where(g):
             block = None
             for k in range(len(steps) - 1, -1, -1):
                 if steps[k][0] != kind:
                     continue
-                block = jnp.int32(steps[k][1]) if block is None else jnp.where(g <= k, steps[k][1], block)
+                cell = steps[k][1][side]
+                block = jnp.int32(cell) if block is None else jnp.where(g <= k, cell, block)
             return (0, block, 0, 0)
 
         return pl.BlockSpec(box, where)
@@ -533,11 +524,13 @@
                 smem,
                 smem,
                 pl.BlockSpec((S, cols), lambda g: (0, 0)),
-                boxes_of("a"),
-                boxes_of("b"),
+                boxes_of("a", 0),
+                boxes_of("a", -1),
+                boxes_of("b", 0),
             ],
-            out_specs=pl.BlockSpec((S, cols), lambda g: (0, 0)),
+            out_specs=pl.BlockSpec(memory_space=pltpu.VMEM),
             scratch_shapes=[
+                f32(BOX, BOX),
                 f32(BOX, BOX),
                 f32(S, cols),
                 f32(S, cols),
@@ -551,8 +544,8 @@
                 f32(S, 4 * LANES),
                 f32(S, 4 * LANES),
                 f32(S, LANES),
-                dma((3,)),
-                dma((3,)),
+                dma((2 + per_dev,)),
+                dma((2 + per_dev,)),
                 dma((2 + per_dev,)),
                 dma((2 + per_dev,)),
                 dma((len(units), 4)),
@@ -561,12 +554,12 @@
                 dma((3,)),
             ],
         ),
-        out_shape=jax.ShapeDtypeStruct((S, cols), jnp.float32),
+        out_shape=pltpu.VMEM((S, cols), jnp.float32),
         compiler_params=pltpu.CompilerParams(
             vmem_limit_bytes=56 * 1024 * 1024, collective_id=0, has_side_effects=True
         ),
         name="transport",
-    )(*[x.swapaxes(1, 2) for x in (shifts_a, widths_a, shifts_b, widths_b)], source, boxes_a, boxes_b)
+    )(*[x.swapaxes(1, 2) for x in (shifts_a, widths_a, shifts_b, widths_b)], source, boxes_a, boxes_a, boxes_b)
 
 
 def solution(mesh):

time: 60.1 us -> 54.7 us (0.910)
  Pallas kernels: 57.6 us -> 53.6 us
  local copies, waits for them, and re-layouts: 2.31 us -> 0.97 us
    pallas_call x1, Pallas kernels: 57.6 us -> 53.6 us  [on_device(): pl.pallas_call(functools.partial(kernel, per_dev, n_row, n_col), grid_spe...]
    unnamed x1, local copies, waits for them, and re-layouts: 2.31 us -> 0.97 us
where the time goes in v2:
time: 54.7 us; the launch traced here: 54.6 us
  Pallas kernels  53.6 us (98%)
  local copies, waits for them, and re-layouts  0.97 us (2%)
    pallas_call x1, Pallas kernels, on_device(): pl.pallas_call(functools.partial(kernel, per_dev, n_row, n_col), grid_spe...  53.6 us

profile of v2, /device:TPU:0, one launch (start us, length us, event | category | flops | bytes accessed | tf_op | source)
XLA Modules:
  0.0 54.6 jit_solution(11165559629160964766)
XLA Ops:
  0.0 53.6 %transport.1 = f32[256,1024]{1,0:T(8,128)S(1)} custom-call(s32[1,2,4]{2,1,0:T(2,128)} %bitcast.4, s32[1,2,4]{2,1,0:T(2,128)} %bitcast.5, s32[1,2,4]{2,1,0:T(2,128)} %bitcast.6, s32[1,2,4]{2,1,0:T(2,128)} %bitcast.7, f32[256,1024]{1,0:T(8,128)} %src.1, f32[1,4,512,512]{3,2,1,0:T(8,128)} %box_c.1, f32[1,4,512,512]{3,2,1,0:T(8,128)} %box_c.1, ...), custom_call_target="tpu_custom_call" | custom-call | tf_op jit(solution)/shard_map/transport/pallas_call | solution.py:516
  53.6 1.0 %copy.9 = f32[256,1024]{1,0:T(8,128)} copy(f32[256,1024]{1,0:T(8,128)S(1)} %transport.1) | data formatting | bytes 2097152

commit v3 on v2

--- a/solution.py
+++ b/solution.py
@@ -88,7 +88,7 @@
 def plan_of(per_dev):
     last = per_dev - 1
     a_order = list(dict.fromkeys([0, last, min(1, last)] + list(range(per_dev - 2, 1, -1))))
-    b_order = list(dict.fromkeys([last, 0] + list(range(per_dev - 2, 0, -1))))
+    b_order = list(dict.fromkeys([last, last - 1, 0] + list(range(per_dev - 3, 0, -1))))
     steps = [("a", tuple(a_order[k : k + 2])) for k in range(0, per_dev, 2)]
     steps += [("b", (j,)) for j in b_order]
     n_tiles = 2 * per_dev + 3
@@ -420,26 +420,32 @@
         def _():
             final = [n for n, u_ in enumerate(units) if u_[0] == n_steps - 1]
             early = [n for n in range(len(units)) if n not in final]
-            fold(early[0])
+            first = 2 * per_dev
+            ready = set()
+
+            def settle(need):
+                while not need <= ready:
+                    n = early.pop(0)
+                    fold(n)
+                    ready.update(range(units[n][1], units[n][1] + units[n][2]))
+
+            settle({n_tiles - 1})
             for n in final:
                 hand_on(n)
-            for n in early[1:]:
-                fold(n)
-
-            first = 2 * per_dev
+            settle(set(range(first - 1, n_tiles)))
             sb[:, 2 * LANES : 3 * LANES] = smooth(first + 2, 1)
             sb[:, : 2 * LANES] = smooth(first, 2)
+            beside(0).start()
+            settle({0})
             over = split(canvas[OWN, tiles(n_tiles - 1, 1)])
             under = split(canvas[OWN, tiles(0, 1)])
             sb[:, tip] = dot_split(over, [b[:LANES, :LANES] for b in (band_hi, band_lo)]) + dot_split(
                 under, [b[2 * LANES : 3 * LANES, :LANES] for b in (band_hi, band_lo)]
             )
-            for k in range(sides):
+            for k in range(1, sides):
                 beside(k).start()
-
-            ready = set()
-            for n in early:
-                ready.update(range(units[n][1], units[n][1] + units[n][2]))
+            while early:
+                settle({units[early[0]][1]})
             shown = set()
 
             def show():

time: 54.7 us -> 53.3 us (0.974)
  Pallas kernels: 53.6 us -> 52.2 us
    pallas_call x1, Pallas kernels: 53.6 us -> 52.2 us  [on_device(): pl.pallas_call(functools.partial(kernel, per_dev, n_row, n_col), grid_spe...]
where the time goes in v3:
time: 53.3 us; the launch traced here: 53.1 us
  Pallas kernels  52.2 us (98%)
  local copies, waits for them, and re-layouts  0.97 us (2%)
    pallas_call x1, Pallas kernels, on_device(): pl.pallas_call(functools.partial(kernel, per_dev, n_row, n_col), grid_spe...  52.2 us

profile of v3, /device:TPU:0, one launch (start us, length us, event | category | flops | bytes accessed | tf_op | source)
XLA Modules:
  0.0 53.1 jit_solution(3856496075028629450)
XLA Ops:
  0.0 52.2 %transport.1 = f32[256,1024]{1,0:T(8,128)S(1)} custom-call(s32[1,2,4]{2,1,0:T(2,128)} %bitcast.4, s32[1,2,4]{2,1,0:T(2,128)} %bitcast.5, s32[1,2,4]{2,1,0:T(2,128)} %bitcast.6, s32[1,2,4]{2,1,0:T(2,128)} %bitcast.7, f32[256,1024]{1,0:T(8,128)} %src.1, f32[1,4,512,512]{3,2,1,0:T(8,128)} %box_c.1, f32[1,4,512,512]{3,2,1,0:T(8,128)} %box_c.1, ...), custom_call_target="tpu_custom_call" | custom-call | tf_op jit(solution)/shard_map/transport/pallas_call | solution.py:522
  52.2 1.0 %copy.9 = f32[256,1024]{1,0:T(8,128)} copy(f32[256,1024]{1,0:T(8,128)S(1)} %transport.1) | data formatting | bytes 2097152

commit v4 on v3

--- a/solution.py
+++ b/solution.py
@@ -71,10 +71,10 @@
     return x.astype(jnp.bfloat16)
 
 
-def target_of(box_ref, height, width):
+def target_of(box, height, width):
     rows = lax.broadcasted_iota(jnp.int32, (BOX, BOX), 0)
     cols = lax.broadcasted_iota(jnp.int32, (BOX, BOX), 1)
-    return jnp.where((rows < height) & (cols < width), box_ref[0, 0], 0.0)
+    return jnp.where((rows < height) & (cols < width), box, 0.0)
 
 
 MESH = pl.DeviceIdType.MESH
@@ -122,11 +122,12 @@
     widths_a,
     shifts_b,
     widths_b,
+    src_hbm,
+    hbm_a,
+    hbm_b,
+    out,
     src,
-    box_a,
-    box_c,
-    box_b,
-    out,
+    boxes,
     tgt,
     tgt_c,
     u_loc,
@@ -149,6 +150,7 @@
     x_recv,
     c_send,
     c_recv,
+    b_sem,
 ):
     g = pl.program_id(0)
     cols = per_dev * S
@@ -167,6 +169,18 @@
 
     j, j_c = pick([c[0] for _, c in steps]), pick([c[-1] for _, c in steps])
     is_a = pick([int(k == "a") for k, _ in steps]) == 1
+    slots, held = [], []
+    for kind, pair in steps:
+        slots.append(range(len(held), len(held) + len(pair)))
+        held += [(kind, i) for i in pair]
+    slot, slot_c = pick([k[0] for k in slots]), pick([k[-1] for k in slots])
+
+    def fetch(k):
+        if k == len(held):
+            return pltpu.make_async_copy(src_hbm, src, b_sem.at[k])
+        kind, i = held[k]
+        hbm = hbm_a if kind == "a" else hbm_b
+        return pltpu.make_async_copy(hbm.at[0, i], boxes.at[k], b_sem.at[k])
 
     def at(dr, dc):
         return (lax.rem(row + dr + n_row, n_row), lax.rem(col + dc + n_col, n_col))
@@ -295,20 +309,38 @@
         def _():
             for dr, dc in peers:
                 pl.semaphore_signal(barrier, inc=1, device_id=at(dr, dc), device_id_type=MESH)
-            mv_s[upper, : cols - HALF] = src[lower, HALF:]
+            for k in slots[0]:
+                fetch(k).start()
+            fetch(len(held)).start()
+            for k in range(slots[1][0], len(held)):
+                fetch(k).start()
             canvas[...] = jnp.zeros_like(canvas)
             band_hi[...], band_lo[...] = the_band()
 
         cells = []
-        for c, box, t in ((j, box_a, tgt), (j_c, box_c, tgt_c)):
+        for c in (j, j_c):
             o_r, o_c = shifts_a[0, 0, c], shifts_a[0, 1, c]
-            h, w = widths_a[0, 0, c], widths_a[0, 1, c]
             krt, kc = gauss_t(o_r), gauss(o_c)
-            t[...] = target_of(box, h, w)
-            here = pl.ds(pl.multiple_of(c * S, S), S)
             in_r = bf(jnp.sum(krt.astype(jnp.float32), axis=1, keepdims=True)).astype(jnp.float32)
             in_c = jnp.sum(kc.astype(jnp.float32), axis=0, keepdims=True)
-            cells.append((gauss(o_r), krt, kc, t, src[:, here], here, in_r * in_c))
+            cells.append((gauss(o_r), krt, kc, in_r * in_c))
+
+        for n, (kind, _) in enumerate(steps):
+            if kind == "a":
+
+                @pl.when(g == n)
+                def _():
+                    for k in slots[n]:
+                        fetch(k).wait()
+                    if n == 0:
+                        fetch(len(held)).wait()
+                        mv_s[upper, : cols - HALF] = src[lower, HALF:]
+
+        for n, (c, k, t) in enumerate(((j, slot, tgt), (j_c, slot_c, tgt_c))):
+            t[...] = target_of(boxes[k], widths_a[0, 0, c], widths_a[0, 1, c])
+            here = pl.ds(pl.multiple_of(c * S, S), S)
+            kr, krt, kc, first = cells[n]
+            cells[n] = (kr, krt, kc, t, src[:, here], here, first)
         back = [c[-1] for c in cells]
         for step in range(ITERS):
             v = [bf(c[3][...] / b) for c, b in zip(cells, back)]
@@ -359,6 +391,7 @@
 
             @pl.when(g == k)
             def _():
+                fetch(slots[k][0]).wait()
                 for c in need:
                     mass(c).wait_recv()
                     scale(c).wait_recv()
@@ -368,7 +401,7 @@
         kr = gauss(o_r)
         krt = gauss_t(o_r)
         kc = gauss(o_c)
-        tgt[...] = target_of(box_b, h, w)
+        tgt[...] = target_of(boxes[slot], h, w)
         here = pl.ds(pl.multiple_of(j * S, S), S)
         a = mv_s[:, here]
         u = mv_u[:, here]
@@ -504,20 +537,6 @@
     steps, units = plan_of(per_dev)
     f32 = lambda *shape: pltpu.VMEM(shape, jnp.float32)
     dma = pltpu.SemaphoreType.DMA
-    box = (1, 1, BOX, BOX)
-
-    def boxes_of(kind, side):
-        def where(g):
-            block = None
-            for k in range(len(steps) - 1, -1, -1):
-                if steps[k][0] != kind:
-                    continue
-                cell = steps[k][1][side]
-                block = jnp.int32(cell) if block is None else jnp.where(g <= k, cell, block)
-            return (0, block, 0, 0)
-
-        return pl.BlockSpec(box, where)
-
     smem = pl.BlockSpec(memory_space=pltpu.SMEM)
     return pl.pallas_call(
         functools.partial(kernel, per_dev, n_row, n_col),
@@ -529,13 +548,12 @@
                 smem,
                 smem,
                 smem,
-                pl.BlockSpec((S, cols), lambda g: (0, 0)),
-                boxes_of("a", 0),
-                boxes_of("a", -1),
-                boxes_of("b", 0),
+                *[pl.BlockSpec(memory_space=pl.ANY)] * 3,
             ],
             out_specs=pl.BlockSpec(memory_space=pltpu.VMEM),
             scratch_shapes=[
+                f32(S, cols),
+                f32(2 * per_dev, BOX, BOX),
                 f32(BOX, BOX),
                 f32(BOX, BOX),
                 f32(S, cols),
@@ -558,6 +576,7 @@
                 dma((len(units), 4)),
                 dma((3,)),
                 dma((3,)),
+                dma((2 * per_dev + 1,)),
             ],
         ),
         out_shape=pltpu.VMEM((S, cols), jnp.float32),
@@ -565,7 +584,7 @@
             vmem_limit_bytes=56 * 1024 * 1024, collective_id=0, has_side_effects=True
         ),
         name="transport",
-    )(*[x.swapaxes(1, 2) for x in (shifts_a, widths_a, shifts_b, widths_b)], source, boxes_a, boxes_a, boxes_b)
+    )(*[x.swapaxes(1, 2) for x in (shifts_a, widths_a, shifts_b, widths_b)], source, boxes_a, boxes_b)
 
 
 def solution(mesh):

time: 53.3 us -> 51.7 us (0.970)
  Pallas kernels: 52.2 us -> 50.3 us
    pallas_call x1, Pallas kernels: 52.2 us -> 50.3 us  [on_device(): pl.pallas_call(functools.partial(kernel, per_dev, n_row, n_col), grid_spe...]
where the time goes in v4:
time: 51.7 us; the launch traced here: 51.3 us
  Pallas kernels  50.3 us (97%)
  local copies, waits for them, and re-layouts  0.97 us (2%)
    pallas_call x1, Pallas kernels, on_device(): pl.pallas_call(functools.partial(kernel, per_dev, n_row, n_col), grid_spe...  50.3 us

profile of v4, /device:TPU:0, one launch (start us, length us, event | category | flops | bytes accessed | tf_op | source)
XLA Modules:
  0.0 51.3 jit_solution(11406596444449272547)
XLA Ops:
  0.0 50.3 %transport.1 = f32[256,1024]{1,0:T(8,128)S(1)} custom-call(s32[1,2,4]{2,1,0:T(2,128)} %bitcast.4, s32[1,2,4]{2,1,0:T(2,128)} %bitcast.5, s32[1,2,4]{2,1,0:T(2,128)} %bitcast.6, s32[1,2,4]{2,1,0:T(2,128)} %bitcast.7, f32[256,1024]{1,0:T(8,128)} %src_hbm.1, f32[1,4,512,512]{3,2,1,0:T(8,128)} %hbm_a.1, f32[1,4,512,512]{3,2,1,0:T(8,128)} %hbm_b.1), custom_call_target="tpu_custom_call" | custom-call | tf_op jit(solution)/shard_map/transport/pallas_call | solution.py:541
  50.3 1.0 %copy.9 = f32[256,1024]{1,0:T(8,128)} copy(f32[256,1024]{1,0:T(8,128)S(1)} %transport.1) | data formatting | bytes 2097152

commit v5 on v4

--- a/solution.py
+++ b/solution.py
@@ -64,7 +64,8 @@
 
 def dot_split(a, b):
     (ah, al), (bh, bl) = a, b
-    return dot(ah, bh) + (dot(ah, bl) + dot(al, bh))
+    both = dot(jnp.concatenate([ah, al], axis=0), bh)
+    return both[: ah.shape[0]] + (both[ah.shape[0] :] + dot(ah, bl))
 
 
 def bf(x):
@@ -418,17 +419,21 @@
         m = lax.broadcasted_iota(jnp.int32, (LANES, 3 * LANES), 1) - 2 * LANES
         weights = split(blur_weight(HALF + o_r + m - r))
         halves = split(plan)
+        none = jnp.zeros((LANES, LANES), jnp.bfloat16)
+        weights = [
+            jnp.concatenate(
+                [jnp.concatenate([x, none], axis=1), jnp.concatenate([none, x], axis=1)], axis=0
+            )
+            for x in weights
+        ]
         parts = []
-        for b in range(-(-TALL // LANES)):
-            height = min(LANES, TALL - b * LANES)
-            lo, hi = max(b - 2, 0), min(b + 1, BOX // LANES)
-            wt = slice((lo - b + 2) * LANES, (hi - b + 2) * LANES)
-            parts.append(
-                dot_split(
-                    [x[:height, wt] for x in weights],
-                    [x[lo * LANES : hi * LANES] for x in halves],
-                )
-            )
+        for b in range(-(-TALL // S)):
+            height = min(S, TALL - b * S)
+            lo, hi = max(2 * b - 2, 0), min(2 * b + 2, BOX // LANES)
+            wt = slice((lo - 2 * b + 2) * LANES, (hi - 2 * b + 2) * LANES)
+            fine, rest = [x[:height, wt] for x in weights]
+            top, low = [x[lo * LANES : hi * LANES] for x in halves]
+            parts.append(dot_split((fine, rest), (top, low)))
         rowed = jnp.concatenate(parts, axis=0)
         s = HALF + o_c
         lane = lax.broadcasted_iota(jnp.int32, (TALL, LANES), 1)

time: 51.7 us -> 51.5 us (level)
  no operation moved by 1% of the time
where the time goes in v5:
time: 51.5 us; the launch traced here: 51.1 us
  Pallas kernels  50.2 us (97%)
  local copies, waits for them, and re-layouts  0.97 us (2%)
    pallas_call x1, Pallas kernels, on_device(): pl.pallas_call(functools.partial(kernel, per_dev, n_row, n_col), grid_spe...  50.2 us

profile of v5, /device:TPU:0, one launch (start us, length us, event | category | flops | bytes accessed | tf_op | source)
XLA Modules:
  0.0 51.1 jit_solution(362521997292325584)
XLA Ops:
  0.0 50.2 %transport.1 = f32[256,1024]{1,0:T(8,128)S(1)} custom-call(s32[1,2,4]{2,1,0:T(2,128)} %bitcast.4, s32[1,2,4]{2,1,0:T(2,128)} %bitcast.5, s32[1,2,4]{2,1,0:T(2,128)} %bitcast.6, s32[1,2,4]{2,1,0:T(2,128)} %bitcast.7, f32[256,1024]{1,0:T(8,128)} %src_hbm.1, f32[1,4,512,512]{3,2,1,0:T(8,128)} %hbm_a.1, f32[1,4,512,512]{3,2,1,0:T(8,128)} %hbm_b.1), custom_call_target="tpu_custom_call" | custom-call | tf_op jit(solution)/shard_map/transport/pallas_call | solution.py:546
  50.2 1.0 %copy.9 = f32[256,1024]{1,0:T(8,128)} copy(f32[256,1024]{1,0:T(8,128)S(1)} %transport.1) | data formatting | bytes 2097152
